TPU v7x, 128 devices: a whole 4x4x4 slice. The times are simulated.
128 devices in a mesh: row: 8 (over z, core), col: 16 (over y, x).
Axes of the slice: x: 4, y: 4, z: 4, core: 2. Of those that a mesh axis runs over, the one named last changes fastest.
Arguments:
- kernel: float32 [16384, 16384], P('row', 'col'), may hold values from 0 to 3, as said below
Outputs:
- trailing: float32 [16384, 16384], P('row', 'col')
- factor_t: float32 [1024, 16384], P('col', 'row')
Inputs may be any that keep to these rules, and one draw needn't show every extreme that they name: K is symmetric: an RBF kernel over 256 donor features plus each donor's noise variance, of 0.5 or more, on the diagonal.
All inputs are finite; a program needn't handle non-finite values.
Results may differ from a plain program's by a relative error of at most 0.0003.
Values sent between devices are 32-bit elements; how exact they have to be, the bound alone decides.
A program may use at most 128 MiB of HBM per device.

v0:
```python
import jax
import jax.numpy as jnp
from jax import lax
from jax.sharding import PartitionSpec as P

PANEL = 512
PANELS = 2


def from_root(value, axis, source):
    kept = jnp.where(lax.axis_index(axis) == source, value, 0).astype(value.dtype)
    return lax.psum(kept, axis)


def outer_update(left_fac, right_fac):
    return lax.dot_general(
        left_fac,
        right_fac,
        (((0,), (0,)), ((), ())),
        precision=lax.Precision.HIGHEST,
        preferred_element_type=jnp.float32,
    )


def local(kernel):
    grid_rows = lax.axis_size("row")
    grid_cols = lax.axis_size("col")
    my_row = lax.axis_index("row")
    my_col = lax.axis_index("col")
    rows_loc = kernel.shape[0]
    cols_loc = kernel.shape[1]
    tile_w = PANEL // grid_cols
    spread = grid_cols // grid_rows
    row_local = jnp.arange(rows_loc, dtype=jnp.int32)
    row_ids = (row_local // tile_w * grid_rows + my_row) * tile_w + row_local % tile_w
    col_local = jnp.arange(cols_loc, dtype=jnp.int32)
    col_ids = (col_local // tile_w * grid_cols + my_col) * tile_w + col_local % tile_w
    down_list = []
    schur = kernel
    for panel_idx in range(PANELS):
        column_tile = schur[:, panel_idx * tile_w : (panel_idx + 1) * tile_w]
        first_col = panel_idx * PANEL
        first_tile = panel_idx * spread
        corner = column_tile[first_tile * tile_w : (first_tile + spread) * tile_w]
        flat_block = corner.reshape(1, spread * tile_w * tile_w)
        blocks = lax.all_gather(flat_block, ("row", "col"), axis=0, tiled=True)
        blocks = blocks.reshape(grid_rows, grid_cols, spread, tile_w, tile_w)
        blocks = blocks.transpose(2, 0, 3, 1, 4).reshape(PANEL, PANEL)
        lower_fac = jnp.linalg.cholesky(blocks)
        columns_t = column_tile.T
        gathered = lax.all_gather(columns_t, "col", axis=0, tiled=True)
        factor_loc = jax.scipy.linalg.solve_triangular(lower_fac, gathered, lower=True)
        factor_loc = jnp.where(row_ids[None, :] >= first_col, factor_loc, 0.0)
        picked = factor_loc.reshape(PANEL, cols_loc // tile_w, spread, tile_w)
        picked = lax.dynamic_index_in_dim(picked, my_col // grid_rows, 2, keepdims=False)
        picked = picked.reshape(PANEL, cols_loc)
        across = from_root(picked, "row", my_col % grid_rows)
        factor_loc, across = (factor_loc, across)
        schur = schur - outer_update(factor_loc, across)
        down_list.append(factor_loc)
    limit = PANELS * PANEL
    keep = (row_ids[:, None] >= limit) & (col_ids[None, :] >= limit)
    trailing = jnp.where(keep, schur, 0.0)
    stacked = jnp.concatenate(down_list, axis=0)
    per_col = PANELS * PANEL // grid_cols
    factor_out = lax.dynamic_slice_in_dim(stacked, my_col * per_col, per_col, 0)
    return (trailing, factor_out)


def solution(mesh):
    return jax.shard_map(
        local,
        mesh=mesh,
        in_specs=(P("row", "col"),),
        out_specs=(P("row", "col"), P("col", "row")),
        check_vma=False,
    )
```

profile of v0, /device:TPU:0, one launch (start us, length us, event | category | flops | bytes accessed | tf_op | source)
XLA Modules:
  0.0 662.9 jit_solution(6436545868017596230)
XLA Ops:
  8.7 9.1 %copy.22 = f32[2048,1024]{0,1:T(8,128)} copy(f32[2048,1024]{1,0:T(8,128)} %param.4) | data formatting | bytes 16777216 | tf_op args[0]
  17.9 1.7 slice_bitcast_fusion.1
  19.7 57.2 %all-gather.11.cloned.1.call-done = f32[128,1,2048]{2,1,0:T(1,128)} async-done(((f32[1,1,2048]{2,1,0:T(1,128)}), f32[128,1,2048]{2,1,0:T(1,128)}) %all-gather.11.cloned.1.call-update) | async-done | bytes 1048592 | tf_op jit(solution)/shard_map/all_gather | solution.py:46
  76.8 3.7 reduce.16
  80.5 2.8 reshape.152
  83.3 5.6 copy.18
  88.9 3.7 reshape.153
  93.2 11.7 %cholesky.286 = f32[128,128]{1,0:T(8,128)S(1)} custom-call(f32[128,128]{1,0:T(8,128)S(1)} %cholesky.426), custom_call_target="Cholesky" | custom-call | tf_op jit(solution)/shard_map/jit(cholesky)/cholesky | solution.py:49
  105.0 9.8 %custom-call.27 = f32[1,128,128]{1,2,0:T(8,128)S(1)} custom-call(f32[1,128,128]{2,1,0:T(8,128)S(1)} %get-tuple-element.65), custom_call_target="InvertDiagBlocksLowerTriangular" | custom-call | tf_op jit(solution)/shard_map/jit(cholesky)/cholesky | solution.py:49
  115.6 11.7 %cholesky.305 = f32[128,128]{1,0:T(8,128)S(1)} custom-call(f32[128,128]{1,0:T(8,128)S(1)} %cholesky.430), custom_call_target="Cholesky" | custom-call | tf_op jit(solution)/shard_map/jit(cholesky)/cholesky | solution.py:49
  127.3 10.0 %custom-call.28 = f32[1,128,128]{1,2,0:T(8,128)S(1)} custom-call(f32[1,128,128]{2,1,0:T(8,128)S(1)} %get-tuple-element.62), custom_call_target="InvertDiagBlocksLowerTriangular" | custom-call | tf_op jit(solution)/shard_map/jit(cholesky)/cholesky | solution.py:49
  138.0 11.7 %cholesky.326 = f32[128,128]{1,0:T(8,128)S(1)} custom-call(f32[128,128]{1,0:T(8,128)S(1)} %cholesky.435), custom_call_target="Cholesky" | custom-call | tf_op jit(solution)/shard_map/jit(cholesky)/cholesky | solution.py:49
  149.7 9.8 %custom-call.29 = f32[1,128,128]{1,2,0:T(8,128)S(1)} custom-call(f32[1,128,128]{2,1,0:T(8,128)S(1)} %get-tuple-element.59), custom_call_target="InvertDiagBlocksLowerTriangular" | custom-call | tf_op jit(solution)/shard_map/jit(cholesky)/cholesky | solution.py:49
  160.2 11.7 %cholesky.343 = f32[128,128]{1,0:T(8,128)S(1)} custom-call(f32[128,128]{1,0:T(8,128)S(1)} %convolution_subtract_fusion.10), custom_call_target="Cholesky" | custom-call | tf_op jit(solution)/shard_map/jit(cholesky)/cholesky | solution.py:49
  176.5 8.2 %while.4 = (s32[]{:T(128)}, f32[512,512]{1,0:T(8,128)S(1)}, s32[4,2]{0,1:T(2,128)S(1)}, f32[4,128,128]{2,1,0:T(8,128)S(1)}, s32[]{:T(128)}) while((s32[]{:T(128)}, f32[512,512]{1,0:T(8,128)S(1)}, s32[4,2]{0,1:T(2,128)S(1)}, f32[4,128,128]{2,1,0:T(8,128)S(1)}, s32[]{:T(128)}) %tuple.58), condition=%wide.while_cond, body=%wide.while_body.sunk | while | flops 2 | bytes 131181 | solution.py:52
  177.6 1.3 bitcast_dynamic-update-slice_fusion.4
  179.5 1.3 bitcast_dynamic-update-slice_fusion.4
  181.5 1.3 bitcast_dynamic-update-slice_fusion.4
  183.4 1.3 bitcast_dynamic-update-slice_fusion.4
  184.8 39.3 %custom-call.30 = f32[4,128,128]{1,2,0:T(8,128)S(1)} custom-call(f32[4,128,128]{2,1,0:T(8,128)S(1)} %get-tuple-element.18), custom_call_target="InvertDiagBlocksLowerTriangular" | custom-call | tf_op jit(solution)/shard_map/jit(_solve_triangular)/triangular_solve | solution.py:52
  224.1 2.4 fusion.26
  226.5 2.2 convolution_subtract_fusion.4
  228.8 1.1 fusion.56
  229.8 1.3 convolution_subtract_fusion.2
  231.1 1.1 fusion.54
  232.2 2.0 fusion.15
  235.3 2.5 maximum_select_fusion
  237.8 5.3 copy.21
  243.1 3.3 dynamic-slice_select_fusion.1
  246.5 63.6 %all-reduce.4.cloned.1.call-done = f32[512,1024]{0,1:T(8,128)} async-done(((f32[512,1024]{0,1:T(8,128)}), f32[512,1024]{0,1:T(8,128)}) %all-reduce.4.cloned.1.call-update) | async-done | bytes 2097168 | tf_op jit(solution)/shard_map/psum | solution.py:12
  310.2 17.0 %convolution_subtract_fusion = f32[2048,1024]{0,1:T(8,128)S(1)} fusion(f32[2048,1024]{0,1:T(8,128)} %copy.22, f32[512,2048]{1,0:T(8,128)} %maximum_select_fusion, f32[512,1024]{0,1:T(8,128)} %all-reduce.4.cloned.1.call-done), kind=kOutput, calls=%fused_computation.9 | convolution fusion | flops 12886999040 | bytes 23068672 | tf_op jit(solution)/shard_map/dot_general | solution.py:16
  327.2 3.4 copy-done
  331.5 1.7 slice_bitcast_fusion
  333.3 61.3 %all-gather.13.cloned.1.call-done = f32[128,1,2048]{2,1,0:T(1,128)} async-done(((f32[1,1,2048]{2,1,0:T(1,128)}), f32[128,1,2048]{2,1,0:T(1,128)}) %all-gather.13.cloned.1.call-update) | async-done | bytes 1048592 | tf_op jit(solution)/shard_map/all_gather | solution.py:46
  394.5 3.7 reduce.17
  398.3 2.7 reshape.156
  401.0 5.6 copy.24
  406.6 3.8 reshape.157
  411.0 11.7 %cholesky.358 = f32[128,128]{1,0:T(8,128)S(1)} custom-call(f32[128,128]{1,0:T(8,128)S(1)} %cholesky.439), custom_call_target="Cholesky" | custom-call | tf_op jit(solution)/shard_map/jit(cholesky)/cholesky | solution.py:49
  422.8 9.8 %custom-call.31 = f32[1,128,128]{1,2,0:T(8,128)S(1)} custom-call(f32[1,128,128]{2,1,0:T(8,128)S(1)} %get-tuple-element.55), custom_call_target="InvertDiagBlocksLowerTriangular" | custom-call | tf_op jit(solution)/shard_map/jit(cholesky)/cholesky | solution.py:49
  433.3 11.7 %cholesky.377 = f32[128,128]{1,0:T(8,128)S(1)} custom-call(f32[128,128]{1,0:T(8,128)S(1)} %cholesky.443), custom_call_target="Cholesky" | custom-call | tf_op jit(solution)/shard_map/jit(cholesky)/cholesky | solution.py:49
  445.1 10.2 %custom-call.32 = f32[1,128,128]{1,2,0:T(8,128)S(1)} custom-call(f32[1,128,128]{2,1,0:T(8,128)S(1)} %get-tuple-element.52), custom_call_target="InvertDiagBlocksLowerTriangular" | custom-call | tf_op jit(solution)/shard_map/jit(cholesky)/cholesky | solution.py:49
  455.9 11.7 %cholesky.398 = f32[128,128]{1,0:T(8,128)S(1)} custom-call(f32[128,128]{1,0:T(8,128)S(1)} %cholesky.448), custom_call_target="Cholesky" | custom-call | tf_op jit(solution)/shard_map/jit(cholesky)/cholesky | solution.py:49
  467.7 9.8 %custom-call.33 = f32[1,128,128]{1,2,0:T(8,128)S(1)} custom-call(f32[1,128,128]{2,1,0:T(8,128)S(1)} %get-tuple-element.49), custom_call_target="InvertDiagBlocksLowerTriangular" | custom-call | tf_op jit(solution)/shard_map/jit(cholesky)/cholesky | solution.py:49
  478.1 11.7 %cholesky.415 = f32[128,128]{1,0:T(8,128)S(1)} custom-call(f32[128,128]{1,0:T(8,128)S(1)} %convolution_subtract_fusion.9), custom_call_target="Cholesky" | custom-call | tf_op jit(solution)/shard_map/jit(cholesky)/cholesky | solution.py:49
  495.0 7.6 %while.5 = (s32[]{:T(128)}, f32[512,512]{1,0:T(8,128)S(1)}, s32[4,2]{0,1:T(2,128)S(1)}, f32[4,128,128]{2,1,0:T(8,128)S(1)}, s32[]{:T(128)}) while((s32[]{:T(128)}, f32[512,512]{1,0:T(8,128)S(1)}, s32[4,2]{0,1:T(2,128)S(1)}, f32[4,128,128]{2,1,0:T(8,128)S(1)}, s32[]{:T(128)}) %tuple.76), condition=%wide.while_cond.clone, body=%wide.while_body.clone.sunk | while | flops 2 | bytes 131181 | solution.py:52
  495.6 1.3 bitcast_dynamic-update-slice_fusion.5
  497.5 1.3 bitcast_dynamic-update-slice_fusion.5
  499.5 1.3 bitcast_dynamic-update-slice_fusion.5
  501.4 1.3 bitcast_dynamic-update-slice_fusion.5
  502.7 39.3 %custom-call.34 = f32[4,128,128]{1,2,0:T(8,128)S(1)} custom-call(f32[4,128,128]{2,1,0:T(8,128)S(1)} %get-tuple-element.19), custom_call_target="InvertDiagBlocksLowerTriangular" | custom-call | tf_op jit(solution)/shard_map/jit(_solve_triangular)/triangular_solve | solution.py:52
  542.0 2.4 fusion.24
  544.4 2.2 convolution_subtract_fusion.3
  547.8 1.3 convolution_subtract_fusion.1
  549.0 1.1 fusion.48
  550.1 2.0 fusion.12
  552.1 1.1 fusion.47
  553.2 2.6 maximum_select_fusion.1
  555.7 5.3 copy.26
  561.1 3.3 dynamic-slice_select_fusion
  564.4 1.9 fusion.30
  566.3 61.8 %all-reduce.6.cloned.1.call-done = f32[512,1024]{0,1:T(8,128)} async-done(((f32[512,1024]{0,1:T(8,128)}), f32[512,1024]{0,1:T(8,128)}) %all-reduce.6.cloned.1.call-update) | async-done | bytes 2097168 | tf_op jit(solution)/shard_map/psum | solution.py:12
  628.2 18.4 %subtract_select_fusion = f32[2048,1024]{0,1:T(8,128)} fusion(f32[2048,1024]{0,1:T(8,128)} %copy-done, pred[2048]{0:T(1024)(128)(4,1)S(1)} %broadcast_compare_fusion.1, pred[1024]{0:T(1024)(128)(4,1)S(1)} %fusion.86, f32[512,2048]{1,0:T(8,128)} %maximum_select_fusion.1, f32[512,1024]{0,1:T(8,128)} %all-reduce.6.cloned.1.call-done), kind=kOutput, calls=%fused_computation.6 | convolution fusion | flops 12891193344 | bytes 23071744 | tf_op jit(solution)/shard_map/dot_general | solution.py:16
  646.5 9.2 %copy.28 = f32[2048,1024]{1,0:T(8,128)} copy(f32[2048,1024]{0,1:T(8,128)} %subtract_select_fusion) | data formatting | bytes 16777216
  (91 shorter events, 20.0 us)
Async XLA Ops:
  7.2 69.7 %all-gather.11.cloned.1.call-start = ((), (), s32[]{:S(2)}) async-start(), calls=%async_computation.4 | async-start | bytes 1056768 | tf_op jit(solution)/shard_map/all_gather | solution.py:46
  8.7 215.4 %all-gather.7.cloned.1.call-start = ((), (), s32[]{:S(2)}) async-start(), calls=%async_computation | async-start | bytes 4456448 | tf_op jit(solution)/shard_map/all_gather | solution.py:51
  19.6 290.6 %all-reduce.4.cloned.1.call-start = ((), (), s32[]{:S(2)}) async-start(), calls=%async_computation.1 | async-start | bytes 4194304 | tf_op jit(solution)/shard_map/psum | solution.py:12
  224.1 5.7 copy-start.1
  246.5 148.0 %all-gather.13.cloned.1.call-start = ((), (), s32[]{:S(2)}) async-start(), calls=%async_computation.5 | async-start | bytes 1056768 | tf_op jit(solution)/shard_map/all_gather | solution.py:46
  327.2 3.4 copy-start
  331.5 210.6 %all-gather.9.cloned.1.call-start = ((), (), s32[]{:S(2)}) async-start(), calls=%async_computation.2 | async-start | bytes 4456448 | tf_op jit(solution)/shard_map/all_gather | solution.py:51
  333.2 295.0 %all-reduce.6.cloned.1.call-start = ((), (), s32[]{:S(2)}) async-start(), calls=%async_computation.3 | async-start | bytes 4194304 | tf_op jit(solution)/shard_map/psum | solution.py:12
  542.0 5.7 copy-start.2
Sparse Core Ops, SparseCore 0:
  10.8 65.9 all-gather.10
  79.5 49.2 all-gather.6
  246.6 63.5 all-reduce.3
  331.6 62.9 all-gather.12
  397.1 49.4 all-gather.8
  564.5 63.6 all-reduce.5
where the time goes:
time: 668 us; the launch traced here: 663 us
  other arithmetic  258 us (39%)
  waiting for transfers between devices  244 us (37%)
  local copies, waits for them, and re-layouts  78.7 us (12%)
  matrix products  61.3 us (9%)
  between operations  19.7 us (3%)
    another operation x29, other arithmetic, local(): lower_fac = jnp.linalg.cholesky(blocks)  158 us
    psum x2, waiting for transfers between devices, from_root(): return lax.psum(kept, axis)  125 us
    all_gather x2, waiting for transfers between devices, local(): blocks = lax.all_gather(flat_block, ('row', 'col'), axis=0, tiled=True)  118 us
    another operation x5, other arithmetic, local(): jax.scipy.linalg.solve_triangular(lower_fac, gathered, lower=True)  78.9 us
    dot_general x2, matrix products, outer_update(): lax.dot_general(left_fac, right_fac, (((0,), (0,)), ((), ())), precision=...  35.4 us
    unnamed x10, local copies, waits for them, and re-layouts  23.1 us
    another operation x14, matrix products, local(): jax.scipy.linalg.solve_triangular(lower_fac, gathered, lower=True)  22.2 us
    another operation x27, local copies, waits for them, and re-layouts, local(): jax.scipy.linalg.solve_triangular(lower_fac, gathered, lower=True)  15.5 us
  transfers between devices with their start and end apart: 6, of which 4 were waited for; matrix products, arithmetic and copies ran while one was open for 46% of the time, Pallas kernels for 0%

commit v1 on v0

--- a/solution.py
+++ b/solution.py
@@ -43,7 +43,10 @@
         first_tile = panel_idx * spread
         corner = column_tile[first_tile * tile_w : (first_tile + spread) * tile_w]
         flat_block = corner.reshape(1, spread * tile_w * tile_w)
-        blocks = lax.all_gather(flat_block, ("row", "col"), axis=0, tiled=True)
+        count = lax.axis_size(("row", "col"))
+        pieces = jnp.stack([flat_block for _ in range(count)])
+        pieces = lax.all_to_all(pieces, ("row", "col"), split_axis=0, concat_axis=0)
+        blocks = jnp.concatenate(pieces, axis=0)
         blocks = blocks.reshape(grid_rows, grid_cols, spread, tile_w, tile_w)
         blocks = blocks.transpose(2, 0, 3, 1, 4).reshape(PANEL, PANEL)
         lower_fac = jnp.linalg.cholesky(blocks)

time: 668 us -> 611 us (0.915)
  waiting for transfers between devices: 244 us -> 167 us
  starting transfers between devices: 0.25 us -> 19.3 us
    all_gather x2 -> x0, waiting for transfers between devices: 118 us -> none  [local(): blocks = lax.all_gather(flat_block, ('row', 'col'), axis=0, tiled=True)]
    all_to_all x0 -> x2, waiting for transfers between devices: none -> 45.7 us  [local(): pieces = lax.all_to_all(pieces, ('row', 'col'), split_axis=0, concat_axis=0)]
    all_to_all x0 -> x2, starting transfers between devices: none -> 19.2 us  [local(): pieces = lax.all_to_all(pieces, ('row', 'col'), split_axis=0, concat_axis=0)]
    another operation x0 -> x6, local copies, waits for them, and re-layouts: none -> 8.74 us  [the longest x2 5.45 us: local(): blocks = blocks.reshape(grid_rows, grid_cols, spread, tile_w, tile_w)]
    all_gather x2 -> x0, other arithmetic: 7.43 us -> none  [local(): blocks = lax.all_gather(flat_block, ('row', 'col'), axis=0, tiled=True)]
    unnamed x10 -> x8, local copies, waits for them, and re-layouts: 23.1 us -> 21.8 us
  transfers between devices with their start and end apart: 6 -> 6, of which waited for: 4 -> 4; matrix products, arithmetic and copies ran while one was open for 46% -> 49% of each run, Pallas kernels for 0% -> 0%
where the time goes in v1:
time: 611 us; the launch traced here: 604 us
  other arithmetic  256 us (42%)
  waiting for transfers between devices  167 us (27%)
  local copies, waits for them, and re-layouts  80.4 us (13%)
  matrix products  61.3 us (10%)
  between operations  19.4 us (3%)
  starting transfers between devices  19.3 us (3%)
    another operation x29, other arithmetic, local(): lower_fac = jnp.linalg.cholesky(blocks)  158 us
    psum x2, waiting for transfers between devices, from_root(): return lax.psum(kept, axis)  122 us
    another operation x5, other arithmetic, local(): jax.scipy.linalg.solve_triangular(lower_fac, gathered, lower=True)  78.9 us
    all_to_all x2, waiting for transfers between devices, local(): pieces = lax.all_to_all(pieces, ('row', 'col'), split_axis=0, concat_axis=0)  45.7 us
    dot_general x2, matrix products, outer_update(): lax.dot_general(left_fac, right_fac, (((0,), (0,)), ((), ())), precision=...  35.4 us
    another operation x14, matrix products, local(): jax.scipy.linalg.solve_triangular(lower_fac, gathered, lower=True)  22.2 us
    unnamed x8, local copies, waits for them, and re-layouts  21.8 us
    all_to_all x2, starting transfers between devices, local(): pieces = lax.all_to_all(pieces, ('row', 'col'), split_axis=0, concat_axis=0)  19.2 us
  transfers between devices with their start and end apart: 6, of which 4 were waited for; matrix products, arithmetic and copies ran while one was open for 49% of the time, Pallas kernels for 0%

profile of v1, /device:TPU:0, one launch (start us, length us, event | category | flops | bytes accessed | tf_op | source)
XLA Modules:
  0.0 604.3 jit_solution(7645060621133841516)
XLA Ops:
  7.2 9.1 %copy.22 = f32[2048,1024]{0,1:T(8,128)} copy(f32[2048,1024]{1,0:T(8,128)} %param.4) | data formatting | bytes 16777216 | tf_op args[0]
  16.3 1.7 slice_bitcast_fusion.1
  18.9 1.5 stack.6
  20.4 11.1 %all-to-all-start = ((f32[128,1,2048]{2,1,0:T(1,128)}), f32[128,1,2048]{2,1,0:T(1,128)S(1)}, u32[]{:S(2)}, u32[]{:S(2)}) async-start(f32[128,1,2048]{2,1,0:T(1,128)} %stack.6), calls=%async_computation | async-start | bytes 2097152 | tf_op jit(solution)/shard_map/all_to_all | solution.py:48
  31.7 22.9 %all-to-all-done = f32[128,1,2048]{2,1,0:T(1,128)S(1)} async-done(((f32[128,1,2048]{2,1,0:T(1,128)}), f32[128,1,2048]{2,1,0:T(1,128)S(1)}, u32[]{:S(2)}, u32[]{:S(2)}) %all-to-all-start) | async-done | bytes 1048608 | tf_op jit(solution)/shard_map/all_to_all | solution.py:48
  54.5 2.5 reduce.16
  57.0 2.8 reshape_reshape.6
  59.8 5.6 copy.18
  65.4 3.8 reshape.147
  69.7 11.7 %cholesky.286 = f32[128,128]{1,0:T(8,128)S(1)} custom-call(f32[128,128]{1,0:T(8,128)S(1)} %cholesky.426), custom_call_target="Cholesky" | custom-call | tf_op jit(solution)/shard_map/jit(cholesky)/cholesky | solution.py:52
  81.5 9.8 %custom-call.27 = f32[1,128,128]{1,2,0:T(8,128)S(1)} custom-call(f32[1,128,128]{2,1,0:T(8,128)S(1)} %get-tuple-element.65), custom_call_target="InvertDiagBlocksLowerTriangular" | custom-call | tf_op jit(solution)/shard_map/jit(cholesky)/cholesky | solution.py:52
  92.1 11.7 %cholesky.305 = f32[128,128]{1,0:T(8,128)S(1)} custom-call(f32[128,128]{1,0:T(8,128)S(1)} %cholesky.430), custom_call_target="Cholesky" | custom-call | tf_op jit(solution)/shard_map/jit(cholesky)/cholesky | solution.py:52
  103.8 10.0 %custom-call.28 = f32[1,128,128]{1,2,0:T(8,128)S(1)} custom-call(f32[1,128,128]{2,1,0:T(8,128)S(1)} %get-tuple-element.62), custom_call_target="InvertDiagBlocksLowerTriangular" | custom-call | tf_op jit(solution)/shard_map/jit(cholesky)/cholesky | solution.py:52
  114.5 11.7 %cholesky.326 = f32[128,128]{1,0:T(8,128)S(1)} custom-call(f32[128,128]{1,0:T(8,128)S(1)} %cholesky.435), custom_call_target="Cholesky" | custom-call | tf_op jit(solution)/shard_map/jit(cholesky)/cholesky | solution.py:52
  126.3 9.8 %custom-call.29 = f32[1,128,128]{1,2,0:T(8,128)S(1)} custom-call(f32[1,128,128]{2,1,0:T(8,128)S(1)} %get-tuple-element.59), custom_call_target="InvertDiagBlocksLowerTriangular" | custom-call | tf_op jit(solution)/shard_map/jit(cholesky)/cholesky | solution.py:52
  136.7 11.7 %cholesky.343 = f32[128,128]{1,0:T(8,128)S(1)} custom-call(f32[128,128]{1,0:T(8,128)S(1)} %convolution_subtract_fusion.10), custom_call_target="Cholesky" | custom-call | tf_op jit(solution)/shard_map/jit(cholesky)/cholesky | solution.py:52
  153.0 8.2 %while.4 = (s32[]{:T(128)}, f32[512,512]{1,0:T(8,128)S(1)}, s32[4,2]{0,1:T(2,128)S(1)}, f32[4,128,128]{2,1,0:T(8,128)S(1)}, s32[]{:T(128)}) while((s32[]{:T(128)}, f32[512,512]{1,0:T(8,128)S(1)}, s32[4,2]{0,1:T(2,128)S(1)}, f32[4,128,128]{2,1,0:T(8,128)S(1)}, s32[]{:T(128)}) %tuple.58), condition=%wide.while_cond, body=%wide.while_body.sunk | while | flops 2 | bytes 131181 | solution.py:55
  154.1 1.3 bitcast_dynamic-update-slice_fusion.4
  156.0 1.3 bitcast_dynamic-update-slice_fusion.4
  158.0 1.3 bitcast_dynamic-update-slice_fusion.4
  159.9 1.3 bitcast_dynamic-update-slice_fusion.4
  161.3 39.3 %custom-call.30 = f32[4,128,128]{1,2,0:T(8,128)S(1)} custom-call(f32[4,128,128]{2,1,0:T(8,128)S(1)} %get-tuple-element.18), custom_call_target="InvertDiagBlocksLowerTriangular" | custom-call | tf_op jit(solution)/shard_map/jit(_solve_triangular)/triangular_solve | solution.py:55
  200.6 2.4 fusion.26
  203.0 2.2 convolution_subtract_fusion.4
  206.4 1.3 convolution_subtract_fusion.2
  208.7 2.0 fusion.15
  210.7 1.1 fusion.53
  211.8 2.5 maximum_select_fusion
  214.3 5.3 copy.21
  219.6 3.3 dynamic-slice_select_fusion.1
  223.1 61.8 %all-reduce.4.cloned.1.call-done = f32[512,1024]{0,1:T(8,128)} async-done(((f32[512,1024]{0,1:T(8,128)}), f32[512,1024]{0,1:T(8,128)}) %all-reduce.4.cloned.1.call-update) | async-done | bytes 2097168 | tf_op jit(solution)/shard_map/psum | solution.py:12
  284.9 17.0 %convolution_subtract_fusion = f32[2048,1024]{0,1:T(8,128)S(1)} fusion(f32[2048,1024]{0,1:T(8,128)} %copy.22, f32[512,2048]{1,0:T(8,128)} %maximum_select_fusion, f32[512,1024]{0,1:T(8,128)} %all-reduce.4.cloned.1.call-done), kind=kOutput, calls=%fused_computation.9 | convolution fusion | flops 12886999040 | bytes 23068672 | tf_op jit(solution)/shard_map/dot_general | solution.py:16
  301.9 3.4 copy-done
  307.0 1.6 stack.7
  308.6 8.0 %all-to-all-start.1 = ((f32[128,1,2048]{2,1,0:T(1,128)}), f32[128,1,2048]{2,1,0:T(1,128)S(1)}, u32[]{:S(2)}, u32[]{:S(2)}) async-start(f32[128,1,2048]{2,1,0:T(1,128)} %stack.7), calls=%async_computation.1 | async-start | bytes 2097152 | tf_op jit(solution)/shard_map/all_to_all | solution.py:48
  316.7 22.8 %all-to-all-done.1 = f32[128,1,2048]{2,1,0:T(1,128)S(1)} async-done(((f32[128,1,2048]{2,1,0:T(1,128)}), f32[128,1,2048]{2,1,0:T(1,128)S(1)}, u32[]{:S(2)}, u32[]{:S(2)}) %all-to-all-start.1) | async-done | bytes 1048608 | tf_op jit(solution)/shard_map/all_to_all | solution.py:48
  339.6 2.5 reduce.17
  342.1 2.7 reshape_reshape.7
  344.8 5.6 copy.24
  350.4 3.8 reshape.149
  354.8 11.7 %cholesky.358 = f32[128,128]{1,0:T(8,128)S(1)} custom-call(f32[128,128]{1,0:T(8,128)S(1)} %cholesky.439), custom_call_target="Cholesky" | custom-call | tf_op jit(solution)/shard_map/jit(cholesky)/cholesky | solution.py:52
  366.6 9.8 %custom-call.31 = f32[1,128,128]{1,2,0:T(8,128)S(1)} custom-call(f32[1,128,128]{2,1,0:T(8,128)S(1)} %get-tuple-element.55), custom_call_target="InvertDiagBlocksLowerTriangular" | custom-call | tf_op jit(solution)/shard_map/jit(cholesky)/cholesky | solution.py:52
  377.1 11.7 %cholesky.377 = f32[128,128]{1,0:T(8,128)S(1)} custom-call(f32[128,128]{1,0:T(8,128)S(1)} %cholesky.443), custom_call_target="Cholesky" | custom-call | tf_op jit(solution)/shard_map/jit(cholesky)/cholesky | solution.py:52
  388.9 10.2 %custom-call.32 = f32[1,128,128]{1,2,0:T(8,128)S(1)} custom-call(f32[1,128,128]{2,1,0:T(8,128)S(1)} %get-tuple-element.52), custom_call_target="InvertDiagBlocksLowerTriangular" | custom-call | tf_op jit(solution)/shard_map/jit(cholesky)/cholesky | solution.py:52
  399.7 11.7 %cholesky.398 = f32[128,128]{1,0:T(8,128)S(1)} custom-call(f32[128,128]{1,0:T(8,128)S(1)} %cholesky.448), custom_call_target="Cholesky" | custom-call | tf_op jit(solution)/shard_map/jit(cholesky)/cholesky | solution.py:52
  411.5 9.8 %custom-call.33 = f32[1,128,128]{1,2,0:T(8,128)S(1)} custom-call(f32[1,128,128]{2,1,0:T(8,128)S(1)} %get-tuple-element.49), custom_call_target="InvertDiagBlocksLowerTriangular" | custom-call | tf_op jit(solution)/shard_map/jit(cholesky)/cholesky | solution.py:52
  421.9 11.7 %cholesky.415 = f32[128,128]{1,0:T(8,128)S(1)} custom-call(f32[128,128]{1,0:T(8,128)S(1)} %convolution_subtract_fusion.9), custom_call_target="Cholesky" | custom-call | tf_op jit(solution)/shard_map/jit(cholesky)/cholesky | solution.py:52
  438.8 7.6 %while.5 = (s32[]{:T(128)}, f32[512,512]{1,0:T(8,128)S(1)}, s32[4,2]{0,1:T(2,128)S(1)}, f32[4,128,128]{2,1,0:T(8,128)S(1)}, s32[]{:T(128)}) while((s32[]{:T(128)}, f32[512,512]{1,0:T(8,128)S(1)}, s32[4,2]{0,1:T(2,128)S(1)}, f32[4,128,128]{2,1,0:T(8,128)S(1)}, s32[]{:T(128)}) %tuple.72), condition=%wide.while_cond.clone, body=%wide.while_body.clone.sunk | while | flops 2 | bytes 131181 | solution.py:55
  439.4 1.3 bitcast_dynamic-update-slice_fusion.5
  441.3 1.3 bitcast_dynamic-update-slice_fusion.5
  443.2 1.3 bitcast_dynamic-update-slice_fusion.5
  445.2 1.3 bitcast_dynamic-update-slice_fusion.5
  446.5 39.3 %custom-call.34 = f32[4,128,128]{1,2,0:T(8,128)S(1)} custom-call(f32[4,128,128]{2,1,0:T(8,128)S(1)} %get-tuple-element.19), custom_call_target="InvertDiagBlocksLowerTriangular" | custom-call | tf_op jit(solution)/shard_map/jit(_solve_triangular)/triangular_solve | solution.py:55
  485.8 2.4 fusion.24
  488.2 2.2 convolution_subtract_fusion.3
  491.5 1.3 convolution_subtract_fusion.1
  493.9 2.0 fusion.12
  497.0 2.6 maximum_select_fusion.1
  499.5 5.3 copy.26
  504.9 3.3 dynamic-slice_select_fusion
  508.2 1.9 fusion.30
  510.1 59.8 %all-reduce.6.cloned.1.call-done = f32[512,1024]{0,1:T(8,128)} async-done(((f32[512,1024]{0,1:T(8,128)}), f32[512,1024]{0,1:T(8,128)}) %all-reduce.6.cloned.1.call-update) | async-done | bytes 2097168 | tf_op jit(solution)/shard_map/psum | solution.py:12
  569.9 18.4 %subtract_select_fusion = f32[2048,1024]{0,1:T(8,128)} fusion(f32[2048,1024]{0,1:T(8,128)} %copy-done, pred[2048]{0:T(1024)(128)(4,1)S(1)} %broadcast_compare_fusion.1, pred[1024]{0:T(1024)(128)(4,1)S(1)} %fusion.86, f32[512,2048]{1,0:T(8,128)} %maximum_select_fusion.1, f32[512,1024]{0,1:T(8,128)} %all-reduce.6.cloned.1.call-done), kind=kOutput, calls=%fused_computation.6 | convolution fusion | flops 12891193344 | bytes 23071744 | tf_op jit(solution)/shard_map/dot_general | solution.py:16
  588.3 9.2 %copy.28 = f32[2048,1024]{1,0:T(8,128)} copy(f32[2048,1024]{0,1:T(8,128)} %subtract_select_fusion) | data formatting | bytes 16777216
  (91 shorter events, 23.3 us)
Async XLA Ops:
  7.2 193.5 %all-gather.3.cloned.1.call-start = ((), (), s32[]{:S(2)}) async-start(), calls=%async_computation.2 | async-start | bytes 4456448 | tf_op jit(solution)/shard_map/all_gather | solution.py:54
  20.4 34.1 %all-to-all-start = ((f32[128,1,2048]{2,1,0:T(1,128)}), f32[128,1,2048]{2,1,0:T(1,128)S(1)}, u32[]{:S(2)}, u32[]{:S(2)}) async-start(f32[128,1,2048]{2,1,0:T(1,128)} %stack.6), calls=%async_computation | async-start | bytes 2097152 | tf_op jit(solution)/shard_map/all_to_all | solution.py:48
  31.5 253.4 %all-reduce.4.cloned.1.call-start = ((), (), s32[]{:S(2)}) async-start(), calls=%async_computation.3 | async-start | bytes 4194304 | tf_op jit(solution)/shard_map/psum | solution.py:12
  200.6 5.7 copy-start.1
  223.0 262.8 %all-gather.5.cloned.1.call-start = ((), (), s32[]{:S(2)}) async-start(), calls=%async_computation.4 | async-start | bytes 4456448 | tf_op jit(solution)/shard_map/all_gather | solution.py:54
  301.9 3.4 copy-start
  308.6 30.9 %all-to-all-start.1 = ((f32[128,1,2048]{2,1,0:T(1,128)}), f32[128,1,2048]{2,1,0:T(1,128)S(1)}, u32[]{:S(2)}, u32[]{:S(2)}) async-start(f32[128,1,2048]{2,1,0:T(1,128)} %stack.7), calls=%async_computation.1 | async-start | bytes 2097152 | tf_op jit(solution)/shard_map/all_to_all | solution.py:48
  316.7 253.3 %all-reduce.6.cloned.1.call-start = ((), (), s32[]{:S(2)}) async-start(), calls=%async_computation.5 | async-start | bytes 4194304 | tf_op jit(solution)/shard_map/psum | solution.py:12
  485.8 5.7 copy-start.2
Sparse Core Ops, SparseCore 0:
  18.2 60.3 all-gather.2
  223.1 61.7 all-reduce.3
  306.2 57.4 all-gather.4
  508.3 61.5 all-reduce.5
